TPU v7x, 32 devices: a whole 2x2x4 slice. The times are simulated.
32 devices in a mesh: prompt: 4 (over z), tensor: 8 (over y, x, core).
Axes of the slice: x: 2, y: 2, z: 4, core: 2. Of those that a mesh axis runs over, the one named last changes fastest.
Arguments:
- embeds: bfloat16 [4, 64, 8192], P('prompt', None, 'tensor'), may hold values from -400 to 400
- norm_gain: bfloat16 [8192], replicated, may hold values from 0.5 to 1.5
- query_weight: bfloat16 [8192, 8192], P('prompt', 'tensor'), may hold values from -1 to 1
- key_weight: bfloat16 [8192, 1024], P('prompt', 'tensor'), may hold values from -6 to 6
- value_weight: bfloat16 [8192, 1024], P('prompt', 'tensor'), may hold values from -0.0625 to 0.0625
- out_weight: bfloat16 [8192, 8192], P('tensor', 'prompt'), may hold values from -0.0625 to 0.0625
- out_grad: bfloat16 [4, 64, 8192], P('prompt', None, 'tensor'), may hold values from -6 to 6
- suffix_pos: int32 [4, 20], P('prompt'), may hold values from 0 to 63
- vocab_table: bfloat16 [65536, 8192], P(('prompt', 'tensor')), may hold values from -0.0625 to 0.0625
- banned: int32 [65536], P(('prompt', 'tensor')), may hold values 0 or 1
Outputs:
- token_scores: float32 [4, 20, 65536], P(None, None, ('prompt', 'tensor'))
All inputs are finite; a program needn't handle non-finite values. No bound on the sum of `banned` on one device may be relied on, other than what follows from the above.
Results may differ from a plain program's by a relative error of at most 0.01.
The roundings to bfloat16 on the way count: a program that leaves them out, or rounds other values in their place, can miss the bound.
Values may be sent and summed in bfloat16 or wider, within the bound.
A program may use at most 192 MiB of HBM per device.

v0:
```python
import math
import jax
import jax.numpy as jnp
from jax import lax
from jax.sharding import PartitionSpec as P

KVH = 8
HD = 128
EPSILON = 1e-05


def dot_f32(spec, a, b):
    return jnp.einsum(spec, a, b, preferred_element_type=jnp.float32)


def on_device(
    embeds,
    norm_gain,
    query_weight,
    key_weight,
    value_weight,
    out_weight,
    out_grad,
    suffix_pos,
    vocab_table,
    banned,
):
    n_prompt = lax.axis_size("prompt")
    n_tensor = lax.axis_size("tensor")
    here_prompt = lax.axis_index("prompt")
    here_tensor = lax.axis_index("tensor")
    seq_len = embeds.shape[1]
    suffix_count = suffix_pos.shape[1]
    width = embeds.shape[2] * n_tensor
    rows_here, head_cols = query_weight.shape
    key_cols = key_weight.shape[1]
    heads_here = head_cols // HD
    slice_width = rows_here // n_tensor
    logit_scale = 1.0 / math.sqrt(HD)
    suffix_all = lax.all_gather(suffix_pos, "prompt", axis=0, tiled=True)
    both = jnp.concatenate([embeds, out_grad], axis=1)
    both = lax.all_gather(both, "tensor", axis=2, tiled=True)
    own = both[:, :seq_len].astype(jnp.float32)
    inverse_norm = lax.rsqrt(jnp.mean(own * own, axis=-1, keepdims=True) + EPSILON)
    inverse_norm = lax.all_gather(inverse_norm, "prompt", axis=0, tiled=True)
    both = lax.all_to_all(both, "prompt", split_axis=2, concat_axis=0, tiled=True)
    embeds = both[:, :seq_len]
    out_grad = both[:, seq_len:]
    embeds_float = embeds.astype(jnp.float32)
    gain_rows = lax.dynamic_slice_in_dim(norm_gain, here_prompt * rows_here, rows_here, 0)
    gain_rows = gain_rows.astype(jnp.float32)
    normed = (embeds_float * inverse_norm * gain_rows).astype(jnp.bfloat16)
    parts = jnp.concatenate(
        [
            dot_f32("psd,dc->psc", normed, query_weight),
            dot_f32("psd,dc->psc", normed, key_weight),
            dot_f32("psd,dc->psc", normed, value_weight),
            dot_f32("psd,cd->psc", out_grad, out_weight),
        ],
        axis=2,
    )
    whole = lax.psum_scatter(parts, "prompt", scatter_dimension=0, tiled=True)
    whole = whole[0].astype(jnp.bfloat16)
    queries = whole[:, :head_cols].reshape(seq_len, heads_here, HD)
    key_values = whole[:, head_cols : head_cols + 2 * key_cols]
    contexts = whole[:, head_cols + 2 * key_cols :].reshape(seq_len, heads_here, HD)
    key_values = lax.all_gather(key_values, "tensor", axis=0, tiled=False)
    key_values = key_values.reshape(n_tensor, seq_len, 2, key_cols).transpose(2, 1, 0, 3)
    key_values = key_values.reshape(2, seq_len, KVH * HD)
    fold = min(heads_here, KVH)
    first = here_tensor * heads_here % KVH * HD
    if fold < KVH:
        key_values = lax.dynamic_slice_in_dim(key_values, first, fold * HD, 2)
    key_values = key_values.reshape(2, seq_len, fold, HD)
    if heads_here > fold:
        key_values = jnp.tile(key_values, (1, 1, heads_here // fold, 1))
    keys, values = (key_values[0], key_values[1])
    logits = dot_f32("qhd,khd->hqk", queries, keys) * logit_scale
    row_index = lax.broadcasted_iota(jnp.int32, (seq_len, seq_len), 0)
    col_index = lax.broadcasted_iota(jnp.int32, (seq_len, seq_len), 1)
    causal = col_index <= row_index
    largest = jnp.max(jnp.where(causal, logits, -1e30), axis=-1, keepdims=True)
    raised = jnp.where(causal, jnp.exp(logits - largest), 0.0)
    probs = raised / jnp.sum(raised, axis=-1, keepdims=True)
    probs_low = probs.astype(jnp.bfloat16)
    prob_grad = dot_f32("qhd,khd->hqk", contexts, values)
    logit_grad = (
        probs * (prob_grad - jnp.sum(prob_grad * probs, axis=-1, keepdims=True)) * logit_scale
    ).astype(jnp.bfloat16)
    steps_iota = lax.broadcasted_iota(jnp.int32, (suffix_count, seq_len), 1)
    chooser = (steps_iota == suffix_pos[0][:, None]).astype(jnp.bfloat16)
    logit_rows = dot_f32("ns,hsk->hnk", chooser, logit_grad).astype(jnp.bfloat16)
    query_grad = dot_f32("hnk,khd->nhd", logit_rows, keys).astype(jnp.bfloat16)
    query_grad = query_grad.reshape(suffix_count, head_cols)
    logit_cols = dot_f32("hqk,nk->hnq", logit_grad, chooser).astype(jnp.bfloat16)
    prob_cols = dot_f32("hqk,nk->hnq", probs_low, chooser).astype(jnp.bfloat16)
    key_each = dot_f32("hnq,qhd->nhd", logit_cols, queries)
    value_each = dot_f32("hnq,qhd->nhd", prob_cols, contexts)
    slots = jnp.stack([key_each, value_each])
    slots = slots.reshape(2, suffix_count, heads_here // fold, fold * HD).sum(axis=2)
    if fold < KVH:
        slots = lax.dynamic_update_slice_in_dim(
            jnp.zeros((2, suffix_count, KVH * HD), jnp.float32), slots, first, 2
        )
    grads = lax.psum_scatter(slots, "tensor", scatter_dimension=2, tiled=True)
    grads = grads.astype(jnp.bfloat16)
    grads = jnp.concatenate([query_grad, grads[0], grads[1]], axis=1)
    grads = lax.all_gather(grads, "prompt", axis=0, tiled=True)
    branch = dot_f32("nc,dc->nd", grads[:, :head_cols], query_weight)
    branch = branch + dot_f32("nc,dc->nd", grads[:, head_cols : head_cols + key_cols], key_weight)
    branch = branch + dot_f32("nc,dc->nd", grads[:, head_cols + key_cols :], value_weight)
    share = lax.psum_scatter(branch, "tensor", scatter_dimension=1, tiled=True)
    start = here_tensor * slice_width
    embeds_slice = lax.dynamic_slice_in_dim(embeds, start, slice_width, 2)
    steps_iota = lax.broadcasted_iota(jnp.int32, (n_prompt, suffix_count, seq_len), 2)
    chooser_all = steps_iota == suffix_all[:, :, None]
    embed_rows = dot_f32("pns,psd->pnd", chooser_all.astype(jnp.bfloat16), embeds_slice)
    norm_rows = jnp.sum(
        jnp.where(chooser_all, inverse_norm[:, None, :, 0], 0.0), axis=-1, keepdims=True
    )
    scaled = (embed_rows * norm_rows).reshape(n_prompt * suffix_count, slice_width)
    norm_rows = norm_rows.reshape(n_prompt * suffix_count, 1)
    gain_slice = lax.dynamic_slice_in_dim(gain_rows, start, slice_width, 0)
    weighted = share * gain_slice
    inner = jnp.sum(weighted * scaled, axis=-1, keepdims=True)
    inner = lax.psum(inner, ("prompt", "tensor")) / width
    suffix_grad = (norm_rows * (weighted - scaled * inner)).astype(jnp.bfloat16)
    flat_grads = lax.all_gather(suffix_grad, ("prompt", "tensor"), axis=1, tiled=True)
    scores = -dot_f32("rd,vd->rv", flat_grads, vocab_table)
    scores = scores.reshape(n_prompt, suffix_count, vocab_table.shape[0])
    return jnp.where(banned[None, None, :] == 1, 0.0, scores)


def solution(mesh):
    return jax.shard_map(
        on_device,
        mesh=mesh,
        in_specs=(
            P("prompt", None, "tensor"),
            P(),
            P("prompt", "tensor"),
            P("prompt", "tensor"),
            P("prompt", "tensor"),
            P("tensor", "prompt"),
            P("prompt", None, "tensor"),
            P("prompt", None),
            P(("prompt", "tensor"), None),
            P(("prompt", "tensor")),
        ),
        out_specs=P(None, None, ("prompt", "tensor")),
        check_vma=False,
    )
```

profile of v0, /device:TPU:0, one launch (start us, length us, event | category | flops | bytes accessed | tf_op | source)
XLA Modules:
  0.0 440.1 jit_solution(10545317299658269144)
XLA Ops:
  6.5 1.7 pad_maximum_fusion.1
  8.3 0.0 all-gather.7.cloned.1.call-update
  8.3 31.6 %all-gather.7.cloned.1.call-done = bf16[1,128,8192]{2,1,0:T(8,128)(2,1)} async-done(((bf16[1,128,1024]{2,1,0:T(8,128)(2,1)}), bf16[1,128,8192]{2,1,0:T(8,128)(2,1)}) %all-gather.7.cloned.1.call-update) | async-done | bytes 2097168 | tf_op jit(solution)/shard_map/all_gather | solution.py:42
  39.9 9.5 %copy.48 = bf16[1,128,8192]{1,0,2:T(2,128)(2,1)} copy(bf16[1,128,8192]{2,1,0:T(8,128)(2,1)} %all-gather.7.cloned.1.call-done) | data formatting | bytes 4194304 | tf_op jit(solution)/shard_map/all_gather | solution.py:42
  49.4 0.5 broadcast.47
  49.9 45.2 %reduce.1 = bf16[8192,128]{1,0:T(8,128)(2,1)S(1)} reduce(bf16[8192,1,128]{2,1,0:T(2,128)(2,1)} %bitcast.91, bf16[]{:T(256)} %broadcast.47), dimensions={1}, to_apply=%bitcast.83.reduce_sub_computation | reduce | bytes 4194306
  95.1 2.1 reshape.85
  97.2 4.7 %all-to-all-start = ((bf16[4,2,131072]{2,1,0:T(2,128)(2,1)}), bf16[4,2,131072]{2,1,0:T(2,128)(2,1)S(1)}, u32[]{:S(2)}, u32[]{:S(2)}) async-start(bf16[4,2,131072]{2,1,0:T(2,128)(2,1)} %reshape.85), calls=%async_computation | async-start | bytes 4194304 | tf_op jit(solution)/shard_map/all_to_all | solution.py:46
  101.9 0.6 dynamic-slice
  103.2 0.7 dynamic-slice_convert_fusion
  103.9 1.5 multiply_reduce_fusion
  105.4 0.1 rsqrt_dynamic-update-slice_fusion
  105.5 36.9 %all-reduce = f32[256]{0:T(256)S(1)} all-reduce(f32[256]{0:T(256)S(1)} %rsqrt_dynamic-update-slice_fusion), channel_id=2, replica_groups=mesh['prompt'=4,'tensor'=8] {'prompt'}, use_global_device_ids=true, to_apply=%add | all-reduce | flops 256 | bytes 2048
  142.4 0.1 broadcast_in_dim.54
  142.5 8.3 %all-to-all-done = bf16[4,2,131072]{2,1,0:T(2,128)(2,1)S(1)} async-done(((bf16[4,2,131072]{2,1,0:T(2,128)(2,1)}), bf16[4,2,131072]{2,1,0:T(2,128)(2,1)S(1)}, u32[]{:S(2)}, u32[]{:S(2)}) %all-to-all-start) | async-done | bytes 2097184 | tf_op jit(solution)/shard_map/all_to_all | solution.py:46
  150.8 3.4 reshape.86
  154.1 2.5 copy.67
  156.6 2.7 copy.49
  159.3 1.9 fusion.18
  161.2 0.0 copy-done.1
  161.2 0.1 copy-done.2
  161.3 0.5 fusion.19
  161.8 3.6 fusion.4
  165.4 1.3 fusion.2
  166.7 1.6 pad_maximum_fusion
  168.3 0.0 reduce-scatter.4.cloned.1.call-update
  168.4 0.0 reduce-scatter.6.cloned.1.call-start
  168.4 48.5 %reduce-scatter.4.cloned.1.call-done = f32[1,64,2304]{2,1,0:T(8,128)} async-done(((f32[4,64,2304]{2,1,0:T(8,128)}), f32[1,64,2304]{2,1,0:T(8,128)}) %reduce-scatter.4.cloned.1.call-update) | async-done | bytes 589840 | tf_op jit(solution)/shard_map/reduce_scatter | solution.py:62
  217.0 1.1 convert_bitcast_fusion
  218.1 9.5 %all-gather.1 = bf16[512,256]{1,0:T(8,128)(2,1)S(1)} all-gather(bf16[64,256]{1,0:T(8,128)(2,1)S(1)} %slice.55), channel_id=3, replica_groups=mesh['prompt'=4,'tensor'=8] {'tensor'}, dimensions={0}, use_global_device_ids=true | all-gather | bytes 294912 | tf_op jit(solution)/shard_map/all_gather | solution.py:67
  227.6 0.1 reshape.61
  227.7 0.2 fusion.31
  227.9 0.2 convolution_multiply_fusion
  228.1 0.7 copy-done.4
  228.8 0.8 fusion.85
  229.6 1.4 convolution_bitcast_fusion
  231.0 1.4 convolution_bitcast_fusion.1
  232.4 0.7 maximum_bitcast_fusion
  233.1 0.0 reduce-scatter.6.cloned.1.call-update
  233.2 0.0 reduce-scatter.8.cloned.1.call-start
  233.2 1.7 fusion.14
  235.0 29.7 %reduce-scatter.6.cloned.1.call-done = f32[2,20,128]{2,1,0:T(8,128)} async-done(((f32[2,20,1024]{2,1,0:T(8,128)}), f32[2,20,128]{2,1,0:T(8,128)}) %reduce-scatter.6.cloned.1.call-update) | async-done | bytes 20496 | tf_op jit(solution)/shard_map/reduce_scatter | solution.py:105
  264.6 0.7 convert_element_type.69
  265.4 13.9 %all-gather.3 = bf16[4,20,1280]{2,1,0:T(8,128)(2,1)S(1)} all-gather(bf16[1,20,1280]{2,1,0:T(8,128)(2,1)S(1)} %maximum_bitcast_fusion.1), channel_id=1, replica_groups=mesh['prompt'=4,'tensor'=8] {'prompt'}, dimensions={0}, use_global_device_ids=true | all-gather | bytes 256000 | tf_op jit(solution)/shard_map/all_gather | solution.py:108
  279.3 0.3 fusion.49
  279.6 1.3 fusion.51
  280.9 4.4 %fusion.6 = f32[80,2048]{1,0:T(8,128)} fusion(f32[80,2048]{1,0:T(8,128)S(1)} %fusion.49, f32[80,2048]{1,0:T(8,128)S(1)} %fusion.51, bf16[2048,1024]{1,0:T(8,128)(2,1)} %param.12, bf16[80,1280]{1,0:T(8,128)(2,1)S(1)} %reshape.77), kind=kOutput, calls=%fused_computation.7 | convolution fusion | flops 335872000 | bytes 6324224 | tf_op jit(solution)/shard_map/nc,dc->nd/dot_general | solution.py:13
  285.4 0.0 reduce-scatter.8.cloned.1.call-update
  285.4 0.0 all-gather.9.cloned.1.call-start
  285.5 0.1 dynamic_slice.10
  285.6 11.1 %all-gather.2 = s32[4,1,20]{2,1,0:T(1,128)S(1)} all-gather(s32[1,1,20]{2,1,0:T(1,128)S(1)} %bitcast.112), channel_id=1, replica_groups=mesh['prompt'=4,'tensor'=8] {'prompt'}, dimensions={0}, use_global_device_ids=true | all-gather | bytes 400 | tf_op jit(solution)/shard_map/all_gather | solution.py:40
  296.7 0.2 select_reduce_fusion.1
  296.8 0.1 mul.77
  296.9 0.1 slice.53
  297.0 0.2 convolution_multiply_fusion.1
  297.2 23.2 %reduce-scatter.8.cloned.1.call-done = f32[80,256]{1,0:T(8,128)} async-done(((f32[80,2048]{1,0:T(8,128)}), f32[80,256]{1,0:T(8,128)}) %reduce-scatter.8.cloned.1.call-update) | async-done | bytes 81936 | tf_op jit(solution)/shard_map/reduce_scatter | solution.py:112
  320.5 1.0 multiply_reduce_fusion.2
  321.5 39.4 %psum.7 = f32[80,1]{0,1:T(1,128)S(1)} all-reduce(f32[80,1]{0,1:T(1,128)S(1)} %bitcast.108), channel_id=1, replica_groups=mesh['prompt'=4,'tensor'=8] {'prompt','tensor'}, use_global_device_ids=true, to_apply=%region_9.10 | all-reduce | flops 80 | bytes 640 | tf_op jit(solution)/shard_map/psum | solution.py:126
  360.9 1.6 multiply_convert_fusion.4
  362.5 54.4 %all-gather.9.cloned.1.call-done = bf16[80,8192]{1,0:T(8,128)(2,1)} async-done(((bf16[80,256]{1,0:T(8,128)(2,1)}), bf16[80,8192]{1,0:T(8,128)(2,1)}) %all-gather.9.cloned.1.call-update) | async-done | bytes 1310736 | tf_op jit(solution)/shard_map/all_gather | solution.py:128
  416.9 15.3 %convolution_negate_fusion = f32[80,2048]{1,0:T(8,128)S(1)} fusion(bf16[80,8192]{1,0:T(8,128)(2,1)} %all-gather.9.cloned.1.call-done, bf16[2048,8192]{1,0:T(8,128)(2,1)} %param.18), kind=kOutput, calls=%fused_computation.8 | convolution fusion | flops 2684518400 | bytes 35520512 | tf_op jit(solution)/shard_map/rd,vd->rv/dot_general | solution.py:13
  432.2 0.1 reshape.66
  432.3 0.1 broadcast_select_fusion
  432.4 1.3 copy.63
  (36 shorter events, 0.3 us)
Async XLA Ops:
  6.5 152.8 %copy-start = (bf16[2048,128]{1,0:T(8,128)(2,1)S(1)}, bf16[2048,128]{1,0:T(8,128)(2,1)}, u32[]{:S(2)}) copy-start(bf16[2048,128]{1,0:T(8,128)(2,1)} %param.14) | copy-start | bytes 1572868
  6.5 33.4 %all-gather.7.cloned.1.call-start = ((), (), s32[]{:S(2)}) async-start(), calls=%async_computation.4 | async-start | bytes 2359296 | tf_op jit(solution)/shard_map/all_gather | solution.py:42
  97.2 4.7 %copy-start.8 = (u32[32]{0:T(128)S(1)}, u32[32]{0:T(128)}, u32[]{:S(2)}) copy-start(u32[32]{0:T(128)} %constant.38) | copy-start | bytes 388
  97.2 53.6 %all-to-all-start = ((bf16[4,2,131072]{2,1,0:T(2,128)(2,1)}), bf16[4,2,131072]{2,1,0:T(2,128)(2,1)S(1)}, u32[]{:S(2)}, u32[]{:S(2)}) async-start(bf16[4,2,131072]{2,1,0:T(2,128)(2,1)} %reshape.85), calls=%async_computation | async-start | bytes 4194304 | tf_op jit(solution)/shard_map/all_to_all | solution.py:46
  101.9 115.0 %reduce-scatter.4.cloned.1.call-start = ((), (), s32[]{:S(2)}) async-start(), calls=%async_computation.5 | async-start | bytes 2949120 | tf_op jit(solution)/shard_map/reduce_scatter | solution.py:62
  159.3 1.9 copy-start.1
  159.3 2.0 copy-start.2
  161.8 3.7 copy-start.7
  168.4 96.2 %reduce-scatter.6.cloned.1.call-start = ((), (), s32[]{:S(2)}) async-start(), calls=%async_computation.6 | async-start | bytes 221184 | tf_op jit(solution)/shard_map/reduce_scatter | solution.py:105
  168.4 61.2 %copy-start.6 = (s32[1,20]{1,0:T(1,128)S(1)}, s32[1,20]{1,0:T(1,128)}, u32[]{:S(2)}) copy-start(s32[1,20]{1,0:T(1,128)} %param.17) | copy-start | bytes 244
  227.9 3.1 copy-start.3
  228.1 0.7 copy-start.4
  233.2 87.3 %reduce-scatter.8.cloned.1.call-start = ((), (), s32[]{:S(2)}) async-start(), calls=%async_computation.7 | async-start | bytes 737280 | tf_op jit(solution)/shard_map/reduce_scatter | solution.py:112
  285.4 77.1 %copy-start.5 = (s32[2048]{0:T(1024)S(1)}, s32[2048]{0:T(1024)}, u32[]{:S(2)}) copy-start(s32[2048]{0:T(1024)} %param.19) | copy-start | bytes 24580
  285.4 131.5 %all-gather.9.cloned.1.call-start = ((), (), s32[]{:S(2)}) async-start(), calls=%async_computation.8 | async-start | bytes 1351680 | tf_op jit(solution)/shard_map/all_gather | solution.py:128
Sparse Core Ops, SparseCore 0:
  9.3 30.5 all-gather.6
  168.5 48.4 reduce-scatter.3
  233.3 31.2 reduce-scatter.5
  285.5 34.8 reduce-scatter.7
  362.6 54.2 all-gather.8
where the time goes:
time: 441 us; the launch traced here: 440 us
  waiting for transfers between devices  196 us (44%)
  blocking collectives  111 us (25%)
  other arithmetic  57 us (13%)
  matrix products  33.6 us (8%)
  local copies, waits for them, and re-layouts  24 us (5%)
  between operations  14.1 us (3%)
  starting transfers between devices  4.86 us (1%)
    all_gather x1, waiting for transfers between devices, on_device(): lax.all_gather(suffix_grad, ('prompt', 'tensor'), axis=1, tiled=True)  54.4 us
    reduce_scatter x1, waiting for transfers between devices, on_device(): whole = lax.psum_scatter(parts, 'prompt', scatter_dimension=0, tiled=True)  48.5 us
    unnamed x3, other arithmetic  45.3 us
    psum x1, blocking collectives, on_device(): inner = lax.psum(inner, ('prompt', 'tensor')) / width  39.4 us
    unnamed x1, blocking collectives  36.9 us
    dot_general x14, matrix products, dot_f32(): return jnp.einsum(spec, a, b, preferred_element_type=jnp.float32)  33.6 us
    all_gather x1, waiting for transfers between devices, on_device(): both = lax.all_gather(both, 'tensor', axis=2, tiled=True)  31.6 us
    reduce_scatter x1, waiting for transfers between devices, on_device(): grads = lax.psum_scatter(slots, 'tensor', scatter_dimension=2, tiled=True)  29.7 us
  transfers between devices with their start and end apart: 6, of which 6 were waited for; matrix products, arithmetic and copies ran while one was open for 1% of the time, Pallas kernels for 0%

commit v1 on v0

--- a/solution.py
+++ b/solution.py
@@ -123,7 +123,7 @@
     gain_slice = lax.dynamic_slice_in_dim(gain_rows, start, slice_width, 0)
     weighted = share * gain_slice
     inner = jnp.sum(weighted * scaled, axis=-1, keepdims=True)
-    inner = lax.psum(inner, ("prompt", "tensor")) / width
+    inner = lax.psum(lax.psum(inner, "tensor"), "prompt") / width
     suffix_grad = (norm_rows * (weighted - scaled * inner)).astype(jnp.bfloat16)
     flat_grads = lax.all_gather(suffix_grad, ("prompt", "tensor"), axis=1, tiled=True)
     scores = -dot_f32("rd,vd->rv", flat_grads, vocab_table)

time: 441 us -> 423 us (0.959)
  blocking collectives: 111 us -> 95.3 us
    psum x1 -> x2, blocking collectives: 39.4 us -> 24 us  [on_device(): inner = lax.psum(lax.psum(inner, 'tensor'), 'prompt') / width]
where the time goes in v1:
time: 423 us; the launch traced here: 421 us
  waiting for transfers between devices  192 us (45%)
  blocking collectives  95.3 us (23%)
  other arithmetic  57 us (13%)
  matrix products  33.6 us (8%)
  local copies, waits for them, and re-layouts  24 us (6%)
  between operations  14.1 us (3%)
  starting transfers between devices  4.86 us (1%)
    all_gather x1, waiting for transfers between devices, on_device(): lax.all_gather(suffix_grad, ('prompt', 'tensor'), axis=1, tiled=True)  51.1 us
    reduce_scatter x1, waiting for transfers between devices, on_device(): whole = lax.psum_scatter(parts, 'prompt', scatter_dimension=0, tiled=True)  48.5 us
    unnamed x3, other arithmetic  45.3 us
    unnamed x1, blocking collectives  36.9 us
    dot_general x14, matrix products, dot_f32(): return jnp.einsum(spec, a, b, preferred_element_type=jnp.float32)  33.6 us
    all_gather x1, waiting for transfers between devices, on_device(): both = lax.all_gather(both, 'tensor', axis=2, tiled=True)  31.6 us
    reduce_scatter x1, waiting for transfers between devices, on_device(): grads = lax.psum_scatter(slots, 'tensor', scatter_dimension=2, tiled=True)  29.7 us
    psum x2, blocking collectives, on_device(): inner = lax.psum(lax.psum(inner, 'tensor'), 'prompt') / width  24 us
  transfers between devices with their start and end apart: 6, of which 6 were waited for; matrix products, arithmetic and copies ran while one was open for 1% of the time, Pallas kernels for 0%

profile of v1, /device:TPU:0, one launch (start us, length us, event | category | flops | bytes accessed | tf_op | source)
XLA Modules:
  0.0 421.4 jit_solution(12735539787260669906)
XLA Ops:
  6.5 1.7 pad_maximum_fusion.1
  8.3 0.0 all-gather.7.cloned.1.call-update
  8.3 31.6 %all-gather.7.cloned.1.call-done = bf16[1,128,8192]{2,1,0:T(8,128)(2,1)} async-done(((bf16[1,128,1024]{2,1,0:T(8,128)(2,1)}), bf16[1,128,8192]{2,1,0:T(8,128)(2,1)}) %all-gather.7.cloned.1.call-update) | async-done | bytes 2097168 | tf_op jit(solution)/shard_map/all_gather | solution.py:42
  39.9 9.5 %copy.48 = bf16[1,128,8192]{1,0,2:T(2,128)(2,1)} copy(bf16[1,128,8192]{2,1,0:T(8,128)(2,1)} %all-gather.7.cloned.1.call-done) | data formatting | bytes 4194304 | tf_op jit(solution)/shard_map/all_gather | solution.py:42
  49.4 0.5 broadcast.47
  49.9 45.2 %reduce.1 = bf16[8192,128]{1,0:T(8,128)(2,1)S(1)} reduce(bf16[8192,1,128]{2,1,0:T(2,128)(2,1)} %bitcast.91, bf16[]{:T(256)} %broadcast.47), dimensions={1}, to_apply=%bitcast.83.reduce_sub_computation | reduce | bytes 4194306
  95.1 2.1 reshape.85
  97.2 4.7 %all-to-all-start = ((bf16[4,2,131072]{2,1,0:T(2,128)(2,1)}), bf16[4,2,131072]{2,1,0:T(2,128)(2,1)S(1)}, u32[]{:S(2)}, u32[]{:S(2)}) async-start(bf16[4,2,131072]{2,1,0:T(2,128)(2,1)} %reshape.85), calls=%async_computation | async-start | bytes 4194304 | tf_op jit(solution)/shard_map/all_to_all | solution.py:46
  101.9 0.6 dynamic-slice
  103.2 0.7 dynamic-slice_convert_fusion
  103.9 1.5 multiply_reduce_fusion
  105.4 0.1 rsqrt_dynamic-update-slice_fusion
  105.5 36.9 %all-reduce = f32[256]{0:T(256)S(1)} all-reduce(f32[256]{0:T(256)S(1)} %rsqrt_dynamic-update-slice_fusion), channel_id=2, replica_groups=mesh['prompt'=4,'tensor'=8] {'prompt'}, use_global_device_ids=true, to_apply=%add | all-reduce | flops 256 | bytes 2048
  142.4 0.1 broadcast_in_dim.54
  142.5 8.3 %all-to-all-done = bf16[4,2,131072]{2,1,0:T(2,128)(2,1)S(1)} async-done(((bf16[4,2,131072]{2,1,0:T(2,128)(2,1)}), bf16[4,2,131072]{2,1,0:T(2,128)(2,1)S(1)}, u32[]{:S(2)}, u32[]{:S(2)}) %all-to-all-start) | async-done | bytes 2097184 | tf_op jit(solution)/shard_map/all_to_all | solution.py:46
  150.8 3.4 reshape.86
  154.1 2.5 copy.67
  156.6 2.7 copy.49
  159.3 1.9 fusion.18
  161.2 0.0 copy-done.1
  161.2 0.1 copy-done.2
  161.3 0.5 fusion.19
  161.8 3.6 fusion.4
  165.4 1.3 fusion.2
  166.7 1.6 pad_maximum_fusion
  168.3 0.0 reduce-scatter.4.cloned.1.call-update
  168.4 0.0 reduce-scatter.6.cloned.1.call-start
  168.4 48.5 %reduce-scatter.4.cloned.1.call-done = f32[1,64,2304]{2,1,0:T(8,128)} async-done(((f32[4,64,2304]{2,1,0:T(8,128)}), f32[1,64,2304]{2,1,0:T(8,128)}) %reduce-scatter.4.cloned.1.call-update) | async-done | bytes 589840 | tf_op jit(solution)/shard_map/reduce_scatter | solution.py:62
  217.0 1.1 convert_bitcast_fusion
  218.1 9.5 %all-gather.1 = bf16[512,256]{1,0:T(8,128)(2,1)S(1)} all-gather(bf16[64,256]{1,0:T(8,128)(2,1)S(1)} %slice.55), channel_id=3, replica_groups=mesh['prompt'=4,'tensor'=8] {'tensor'}, dimensions={0}, use_global_device_ids=true | all-gather | bytes 294912 | tf_op jit(solution)/shard_map/all_gather | solution.py:67
  227.6 0.1 reshape.61
  227.7 0.2 fusion.31
  227.9 0.2 convolution_multiply_fusion
  228.1 0.7 copy-done.4
  228.8 0.8 fusion.85
  229.6 1.4 convolution_bitcast_fusion
  231.0 1.4 convolution_bitcast_fusion.1
  232.4 0.7 maximum_bitcast_fusion
  233.1 0.0 reduce-scatter.6.cloned.1.call-update
  233.2 0.0 reduce-scatter.8.cloned.1.call-start
  233.2 1.7 fusion.14
  235.0 29.7 %reduce-scatter.6.cloned.1.call-done = f32[2,20,128]{2,1,0:T(8,128)} async-done(((f32[2,20,1024]{2,1,0:T(8,128)}), f32[2,20,128]{2,1,0:T(8,128)}) %reduce-scatter.6.cloned.1.call-update) | async-done | bytes 20496 | tf_op jit(solution)/shard_map/reduce_scatter | solution.py:105
  264.6 0.7 convert_element_type.69
  265.4 13.9 %all-gather.3 = bf16[4,20,1280]{2,1,0:T(8,128)(2,1)S(1)} all-gather(bf16[1,20,1280]{2,1,0:T(8,128)(2,1)S(1)} %maximum_bitcast_fusion.1), channel_id=1, replica_groups=mesh['prompt'=4,'tensor'=8] {'prompt'}, dimensions={0}, use_global_device_ids=true | all-gather | bytes 256000 | tf_op jit(solution)/shard_map/all_gather | solution.py:108
  279.3 0.3 fusion.49
  279.6 1.3 fusion.51
  280.9 4.4 %fusion.6 = f32[80,2048]{1,0:T(8,128)} fusion(f32[80,2048]{1,0:T(8,128)S(1)} %fusion.49, f32[80,2048]{1,0:T(8,128)S(1)} %fusion.51, bf16[2048,1024]{1,0:T(8,128)(2,1)} %param.12, bf16[80,1280]{1,0:T(8,128)(2,1)S(1)} %reshape.77), kind=kOutput, calls=%fused_computation.7 | convolution fusion | flops 335872000 | bytes 6324224 | tf_op jit(solution)/shard_map/nc,dc->nd/dot_general | solution.py:13
  285.4 0.0 all-gather.9.cloned.1.call-start
  285.5 0.1 dynamic_slice.10
  285.6 11.1 %all-gather.2 = s32[4,1,20]{2,1,0:T(1,128)S(1)} all-gather(s32[1,1,20]{2,1,0:T(1,128)S(1)} %bitcast.112), channel_id=1, replica_groups=mesh['prompt'=4,'tensor'=8] {'prompt'}, dimensions={0}, use_global_device_ids=true | all-gather | bytes 400 | tf_op jit(solution)/shard_map/all_gather | solution.py:40
  296.7 0.2 select_reduce_fusion.1
  296.8 0.1 mul.77
  296.9 0.1 slice.53
  297.0 0.2 convolution_multiply_fusion.1
  297.2 23.2 %reduce-scatter.8.cloned.1.call-done = f32[80,256]{1,0:T(8,128)} async-done(((f32[80,2048]{1,0:T(8,128)}), f32[80,256]{1,0:T(8,128)}) %reduce-scatter.8.cloned.1.call-update) | async-done | bytes 81936 | tf_op jit(solution)/shard_map/reduce_scatter | solution.py:112
  320.5 1.0 multiply_reduce_fusion.2
  321.5 12.3 %psum.14 = f32[80,1]{0,1:T(1,128)S(1)} all-reduce(f32[80,1]{0,1:T(1,128)S(1)} %bitcast.108), channel_id=1, replica_groups=mesh['prompt'=4,'tensor'=8] {'tensor'}, use_global_device_ids=true, to_apply=%region_9.10 | all-reduce | flops 80 | bytes 640 | tf_op jit(solution)/shard_map/psum | solution.py:126
  333.7 11.7 %psum.15 = f32[80,1]{0,1:T(1,128)S(1)} all-reduce(f32[80,1]{0,1:T(1,128)S(1)} %psum.14), channel_id=1, replica_groups=mesh['prompt'=4,'tensor'=8] {'prompt'}, use_global_device_ids=true, to_apply=%region_10.11 | all-reduce | flops 80 | bytes 640 | tf_op jit(solution)/shard_map/psum | solution.py:126
  345.4 1.6 multiply_convert_fusion.4
  347.1 51.1 %all-gather.9.cloned.1.call-done = bf16[80,8192]{1,0:T(8,128)(2,1)} async-done(((bf16[80,256]{1,0:T(8,128)(2,1)}), bf16[80,8192]{1,0:T(8,128)(2,1)}) %all-gather.9.cloned.1.call-update) | async-done | bytes 1310736 | tf_op jit(solution)/shard_map/all_gather | solution.py:128
  398.2 15.3 %convolution_negate_fusion = f32[80,2048]{1,0:T(8,128)S(1)} fusion(bf16[80,8192]{1,0:T(8,128)(2,1)} %all-gather.9.cloned.1.call-done, bf16[2048,8192]{1,0:T(8,128)(2,1)} %param.18), kind=kOutput, calls=%fused_computation.8 | convolution fusion | flops 2684518400 | bytes 35520512 | tf_op jit(solution)/shard_map/rd,vd->rv/dot_general | solution.py:13
  413.5 0.1 reshape.66
  413.5 0.1 broadcast_select_fusion
  413.6 1.3 copy.63
  (37 shorter events, 0.3 us)
Async XLA Ops:
  6.5 152.8 %copy-start = (bf16[2048,128]{1,0:T(8,128)(2,1)S(1)}, bf16[2048,128]{1,0:T(8,128)(2,1)}, u32[]{:S(2)}) copy-start(bf16[2048,128]{1,0:T(8,128)(2,1)} %param.14) | copy-start | bytes 1572868
  6.5 33.4 %all-gather.7.cloned.1.call-start = ((), (), s32[]{:S(2)}) async-start(), calls=%async_computation.4 | async-start | bytes 2359296 | tf_op jit(solution)/shard_map/all_gather | solution.py:42
  97.2 4.7 %copy-start.8 = (u32[32]{0:T(128)S(1)}, u32[32]{0:T(128)}, u32[]{:S(2)}) copy-start(u32[32]{0:T(128)} %constant.38) | copy-start | bytes 388
  97.2 53.6 %all-to-all-start = ((bf16[4,2,131072]{2,1,0:T(2,128)(2,1)}), bf16[4,2,131072]{2,1,0:T(2,128)(2,1)S(1)}, u32[]{:S(2)}, u32[]{:S(2)}) async-start(bf16[4,2,131072]{2,1,0:T(2,128)(2,1)} %reshape.85), calls=%async_computation | async-start | bytes 4194304 | tf_op jit(solution)/shard_map/all_to_all | solution.py:46
  101.9 115.0 %reduce-scatter.4.cloned.1.call-start = ((), (), s32[]{:S(2)}) async-start(), calls=%async_computation.5 | async-start | bytes 2949120 | tf_op jit(solution)/shard_map/reduce_scatter | solution.py:62
  159.3 1.9 copy-start.1
  159.3 2.0 copy-start.2
  161.8 3.7 copy-start.7
  168.4 96.2 %reduce-scatter.6.cloned.1.call-start = ((), (), s32[]{:S(2)}) async-start(), calls=%async_computation.6 | async-start | bytes 221184 | tf_op jit(solution)/shard_map/reduce_scatter | solution.py:105
  168.4 61.2 %copy-start.6 = (s32[1,20]{1,0:T(1,128)S(1)}, s32[1,20]{1,0:T(1,128)}, u32[]{:S(2)}) copy-start(s32[1,20]{1,0:T(1,128)} %param.17) | copy-start | bytes 244
  227.9 3.1 copy-start.3
  228.1 0.7 copy-start.4
  233.2 87.3 %reduce-scatter.8.cloned.1.call-start = ((), (), s32[]{:S(2)}) async-start(), calls=%async_computation.7 | async-start | bytes 737280 | tf_op jit(solution)/shard_map/reduce_scatter | solution.py:112
  285.4 61.7 %copy-start.5 = (s32[2048]{0:T(1024)S(1)}, s32[2048]{0:T(1024)}, u32[]{:S(2)}) copy-start(s32[2048]{0:T(1024)} %param.19) | copy-start | bytes 24580
  285.4 112.8 %all-gather.9.cloned.1.call-start = ((), (), s32[]{:S(2)}) async-start(), calls=%async_computation.8 | async-start | bytes 1351680 | tf_op jit(solution)/shard_map/all_gather | solution.py:128
Sparse Core Ops, SparseCore 0:
  9.3 30.5 all-gather.6
  168.5 48.4 reduce-scatter.3
  233.3 31.2 reduce-scatter.5
  285.5 34.8 reduce-scatter.7
  347.2 50.9 all-gather.8
